TPU v7x, 32 devices: a whole 2x2x4 slice. The times are simulated.
32 devices in a mesh: row: 4 (over z), col: 8 (over y, x, core).
Axes of the slice: x: 2, y: 2, z: 4, core: 2. Of those that a mesh axis runs over, the one named last changes fastest.
Arguments:
- hessian: float32 [18432, 18432], P('row', 'col'), may hold values from -1 to 5, as said below
- right_side: float32 [18432, 512], P('row'), may hold values from -6 to 6
- mask: int32 [18432, 512], P('row'), may hold values 0 or 1
- damping: float32 [1], replicated, may hold values from 0.4 to 1.2
Outputs:
- solution: float32 [18432, 512], P('row')
Inputs may be any that keep to these rules, and one draw needn't show every extreme that they name: hessian is symmetric and positive definite.
All inputs are finite; a program needn't handle non-finite values. No bound on the sum of `mask` on one device may be relied on, other than what follows from the above.
Results may differ from a plain program's by a relative error of at most 0.0001.
Values sent between devices are 32-bit elements; how exact they have to be, the bound alone decides.
No kernel may reach another device: no remote copies, remote signals or barrier semaphores. Data moves between devices by JAX's collectives and lax.ppermute only.
A program may use at most 192 MiB of HBM per device.

v0:
```python
import jax
import jax.numpy as jnp
from jax import lax
from jax.sharding import PartitionSpec as P

ITERS = 3
epsilon = 1e-06


def from_root(block, axis, source):
    block = jnp.where(lax.axis_index(axis) == source, block, jnp.zeros_like(block))
    return lax.psum(block, axis)


def column_sums(first, second):
    return jnp.sum(first * second, axis=0)


def both_sums(residual, applied):
    return lax.psum((column_sums(residual, residual), column_sums(residual, applied)), "row")


def on_device(hessian, right_side, mask, damping):
    mask_float = mask.astype(jnp.float32)
    damping_value = damping[0]
    blocks_ratio = lax.axis_size("col") // lax.axis_size("row")
    block_width = hessian.shape[1]
    col_position = lax.axis_index("col")

    def masked_apply(vector):
        own_slice = lax.dynamic_slice_in_dim(
            vector, col_position % blocks_ratio * block_width, block_width, 0
        )
        column_block = from_root(own_slice, "row", col_position // blocks_ratio)
        partial_value = jnp.dot(
            hessian,
            column_block,
            precision=lax.Precision.HIGHEST,
            preferred_element_type=jnp.float32,
        )
        summed = lax.psum(partial_value, "col")
        return mask_float * (summed + damping_value * vector)

    residual = mask_float * right_side
    direction = residual
    solution = jnp.zeros_like(right_side)
    applied = masked_apply(residual)
    norm_now, inner = both_sums(residual, applied)
    step_size = norm_now / (inner + epsilon)
    along = applied
    for iteration in range(ITERS):
        solution = solution + step_size * direction
        residual = residual - step_size * along
        if iteration + 1 < ITERS:
            applied = masked_apply(residual)
            norm_next, inner = both_sums(residual, applied)
            factor = norm_next / (norm_now + epsilon)
            curvature = inner - factor * norm_next / step_size
            step_size = norm_next / (curvature + epsilon)
            direction = residual + factor * direction
            along = applied + factor * along
            norm_now = norm_next
    return solution


def solution(mesh):
    in_specs = (P("row", "col"), P("row", None), P("row", None), P())
    out_specs = P("row", None)
    return jax.shard_map(
        on_device, mesh=mesh, in_specs=in_specs, out_specs=out_specs, check_vma=False
    )
```

profile of v0, /device:TPU:0, one launch (start us, length us, event | category | flops | bytes accessed | tf_op | source)
XLA Modules:
  0.0 1330.0 jit_solution(18420275999820878551)
XLA Ops:
  6.5 0.0 all-reduce.10.cloned.1.call-start
  6.5 9.6 copy.5
  16.2 9.6 copy.6
  25.7 11.9 convert_multiply_fusion
  37.7 4.9 dynamic-slice_select_fusion.2
  42.6 0.0 all-reduce.10.cloned.1.call-update
  42.6 0.0 all-reduce.12.cloned.1.call-start
  42.6 174.8 %all-reduce.10.cloned.1.call-done = f32[2304,512]{0,1:T(8,128)} async-done(((f32[2304,512]{0,1:T(8,128)}), f32[2304,512]{0,1:T(8,128)}) %all-reduce.10.cloned.1.call-update) | async-done | bytes 4718608 | tf_op jit(solution)/shard_map/psum | solution.py:12
  217.4 75.6 %convolution_bitcast_fusion.2 = f32[4608,512]{0,1:T(8,128)} fusion(f32[2304,512]{0,1:T(8,128)} %all-reduce.10.cloned.1.call-done, f32[4608,2304]{1,0:T(8,128)} %param.4), kind=kOutput, calls=%fused_computation.14 | convolution fusion | flops 65229815808 | bytes 56623104 | tf_op jit(solution)/shard_map/dot_general | solution.py:35
  293.0 0.0 all-reduce.12.cloned.1.call-update
  293.0 0.0 all-reduce.14.cloned.1.call-start
  293.7 136.0 %all-reduce.12.cloned.1.call-done = f32[4608,512]{0,1:T(8,128)} async-done(((f32[4608,512]{0,1:T(8,128)}), f32[4608,512]{0,1:T(8,128)}) %all-reduce.12.cloned.1.call-update) | async-done | bytes 9437200 | tf_op jit(solution)/shard_map/psum | solution.py:41
  429.7 10.3 multiply_reduce_fusion.4
  440.1 11.7 all-reduce.2
  451.8 11.1 multiply_subtract_fusion.1
  462.9 0.0 copy-start
  462.9 3.6 copy-done
  466.6 2.5 dynamic-slice_select_fusion.1
  469.1 0.0 all-reduce.14.cloned.1.call-update
  469.1 0.2 all-reduce.16.cloned.1.call-start
  469.3 169.2 %all-reduce.14.cloned.1.call-done = f32[2304,512]{0,1:T(8,128)} async-done(((f32[2304,512]{0,1:T(8,128)}), f32[2304,512]{0,1:T(8,128)}) %all-reduce.14.cloned.1.call-update) | async-done | bytes 4718608 | tf_op jit(solution)/shard_map/psum | solution.py:12
  638.5 75.6 %convolution_bitcast_fusion.1 = f32[4608,512]{0,1:T(8,128)} fusion(f32[2304,512]{0,1:T(8,128)} %all-reduce.14.cloned.1.call-done, f32[4608,2304]{1,0:T(8,128)} %param.4), kind=kOutput, calls=%fused_computation.13 | convolution fusion | flops 65229815808 | bytes 56623104 | tf_op jit(solution)/shard_map/dot_general | solution.py:35
  714.1 0.0 all-reduce.16.cloned.1.call-update
  714.1 0.0 all-reduce.18.cloned.1.call-start
  714.2 136.7 %all-reduce.16.cloned.1.call-done = f32[4608,512]{0,1:T(8,128)} async-done(((f32[4608,512]{0,1:T(8,128)}), f32[4608,512]{0,1:T(8,128)}) %all-reduce.16.cloned.1.call-update) | async-done | bytes 9437200 | tf_op jit(solution)/shard_map/psum | solution.py:41
  850.9 10.2 multiply_reduce_fusion.2
  861.1 11.7 all-reduce.1
  872.8 15.9 %multiply_subtract_fusion = f32[4608,512]{0,1:T(8,128)S(1)} fusion(f32[4608,512]{0,1:T(8,128)} %copy-done, f32[4608,512]{0,1:T(8,128)} %all-reduce.16.cloned.1.call-done, s32[4608,512]{0,1:T(8,128)} %copy.5, f32[512]{0:T(512)S(1)} %get-tuple-element.21, f32[512]{0:T(512)S(1)} %get-tuple-element.17, f32[]{:T(128)} %bitcast.14, ...), kind=kLoop, calls=%fused_computation.3 | loop fusion | flops 25952256 | bytes 56627204 | tf_op jit(solution)/shard_map/sub | solution.py:53
  888.7 0.0 copy-start.1
  888.7 3.7 copy-done.1
  892.5 2.5 dynamic-slice_select_fusion
  895.0 0.0 all-reduce.18.cloned.1.call-update
  895.0 0.3 all-reduce.20.cloned.1.call-start
  895.3 169.1 %all-reduce.18.cloned.1.call-done = f32[2304,512]{0,1:T(8,128)} async-done(((f32[2304,512]{0,1:T(8,128)}), f32[2304,512]{0,1:T(8,128)}) %all-reduce.18.cloned.1.call-update) | async-done | bytes 4718608 | tf_op jit(solution)/shard_map/psum | solution.py:12
  1064.4 75.6 %convolution_bitcast_fusion = f32[4608,512]{0,1:T(8,128)} fusion(f32[2304,512]{0,1:T(8,128)} %all-reduce.18.cloned.1.call-done, f32[4608,2304]{1,0:T(8,128)} %param.4), kind=kOutput, calls=%fused_computation.12 | convolution fusion | flops 65229815808 | bytes 56623104 | tf_op jit(solution)/shard_map/dot_general | solution.py:35
  1140.0 0.0 all-reduce.20.cloned.1.call-update
  1140.0 136.7 %all-reduce.20.cloned.1.call-done = f32[4608,512]{0,1:T(8,128)} async-done(((f32[4608,512]{0,1:T(8,128)}), f32[4608,512]{0,1:T(8,128)}) %all-reduce.20.cloned.1.call-update) | async-done | bytes 9437200 | tf_op jit(solution)/shard_map/psum | solution.py:41
  1276.8 10.2 multiply_reduce_fusion
  1287.0 11.7 all-reduce
  1298.7 14.8 %multiply_add_fusion = f32[4608,512]{0,1:T(8,128)} fusion(f32[4608,512]{0,1:T(8,128)} %copy-done.1, f32[4608,512]{0,1:T(8,128)} %copy-done, f32[4608,512]{0,1:T(8,128)} %convert_multiply_fusion, f32[512]{0:T(512)S(1)} %get-tuple-element.20, f32[512]{0:T(512)S(1)} %get-tuple-element.19, f32[512]{0:T(512)S(1)} %get-tuple-element.21, ...), kind=kLoop, calls=%fused_computation | loop fusion | flops 21233664 | bytes 37758976 | tf_op jit(solution)/shard_map/add | solution.py:52
  1313.6 9.6 copy.7
  (3 shorter events, 0.0 us)
Async XLA Ops:
  6.5 210.9 %all-reduce.10.cloned.1.call-start = ((), (), s32[]{:S(2)}) async-start(), calls=%async_computation | async-start | bytes 9437184 | tf_op jit(solution)/shard_map/psum | solution.py:12
  42.6 387.1 %all-reduce.12.cloned.1.call-start = ((), (), s32[]{:S(2)}) async-start(), calls=%async_computation.1 | async-start | bytes 18874368 | tf_op jit(solution)/shard_map/psum | solution.py:41
  293.0 345.5 %all-reduce.14.cloned.1.call-start = ((), (), s32[]{:S(2)}) async-start(), calls=%async_computation.2 | async-start | bytes 9437184 | tf_op jit(solution)/shard_map/psum | solution.py:12
  462.9 3.7 copy-start
  469.1 381.8 %all-reduce.16.cloned.1.call-start = ((), (), s32[]{:S(2)}) async-start(), calls=%async_computation.3 | async-start | bytes 18874368 | tf_op jit(solution)/shard_map/psum | solution.py:41
  714.1 350.3 %all-reduce.18.cloned.1.call-start = ((), (), s32[]{:S(2)}) async-start(), calls=%async_computation.4 | async-start | bytes 9437184 | tf_op jit(solution)/shard_map/psum | solution.py:12
  888.7 3.7 copy-start.1
  895.0 381.8 %all-reduce.20.cloned.1.call-start = ((), (), s32[]{:S(2)}) async-start(), calls=%async_computation.5 | async-start | bytes 18874368 | tf_op jit(solution)/shard_map/psum | solution.py:41
Sparse Core Ops, SparseCore 0:
  42.7 174.6 all-reduce.9
  293.1 136.5 all-reduce.11
  469.2 169.2 all-reduce.13
  714.3 136.5 all-reduce.15
  895.1 169.2 all-reduce.17
  1140.2 136.5 all-reduce.19
where the time goes:
time: 1330 us
  waiting for transfers between devices  923 us (69%)
  matrix products  227 us (17%)
  other arithmetic  94.6 us (7%)
  local copies, waits for them, and re-layouts  36.2 us (3%)
  blocking collectives  35.1 us (3%)
  between operations  14.2 us (1%)
    psum x3, waiting for transfers between devices, from_root(): return lax.psum(block, axis)  513 us
    psum x3, waiting for transfers between devices, masked_apply(): summed = lax.psum(partial_value, 'col')  409 us
    dot_general x3, matrix products, masked_apply(): jnp.dot(hessian, column_block, precision=lax.Precision.HIGHEST, preferred...  227 us
    psum x3, blocking collectives, both_sums(): lax.psum((column_sums(residual, residual), column_sums(residual, applied)...  35.1 us
    reduce_sum x3, other arithmetic, column_sums(): return jnp.sum(first * second, axis=0)  30.8 us
    sub x2, other arithmetic, on_device(): residual = residual - step_size * along  27 us
  transfers between devices with their start and end apart: 6, of which 6 were waited for; matrix products, arithmetic and copies ran while one was open for 0% of the time, Pallas kernels for 0%

commit v1 on v0

--- a/solution.py
+++ b/solution.py
@@ -38,7 +38,9 @@
             precision=lax.Precision.HIGHEST,
             preferred_element_type=jnp.float32,
         )
-        summed = lax.psum(partial_value, "col")
+        summed = partial_value
+        for hop in (1, 2, 4):
+            summed = summed + lax.ppermute(summed, "col", [(dev, dev ^ hop) for dev in range(8)])
         return mask_float * (summed + damping_value * vector)
 
     residual = mask_float * right_side

time: 1330 us -> 2280 us (1.71)
  waiting for transfers between devices: 923 us -> 1780 us
  other arithmetic: 94.6 us -> 176 us
    ppermute x0 -> x9, waiting for transfers between devices: none -> 1260 us  [masked_apply(): lax.ppermute(summed, 'col', [(dev, dev ^ hop) for dev in range(8)])]
    psum x3 -> x0, waiting for transfers between devices: 409 us -> none  [masked_apply(): summed = lax.psum(partial_value, 'col')]
    add x0 -> x6, other arithmetic: none -> 70.3 us  [masked_apply(): summed + lax.ppermute(summed, 'col', [(dev, dev ^ hop) for dev in range(8)])]
  transfers between devices with their start and end apart: 6 -> 12, of which waited for: 6 -> 12; matrix products, arithmetic and copies ran while one was open for 0% -> 0% of each run, Pallas kernels for 0% -> 0%
where the time goes in v1:
time: 2280 us
  waiting for transfers between devices  1780 us (78%)
  matrix products  226 us (10%)
  other arithmetic  176 us (8%)
  local copies, waits for them, and re-layouts  43.4 us (2%)
  blocking collectives  28.4 us (1%)
    ppermute x9, waiting for transfers between devices, masked_apply(): lax.ppermute(summed, 'col', [(dev, dev ^ hop) for dev in range(8)])  1260 us
    psum x3, waiting for transfers between devices, from_root(): return lax.psum(block, axis)  515 us
    dot_general x3, matrix products, masked_apply(): jnp.dot(hessian, column_block, precision=lax.Precision.HIGHEST, preferred...  226 us
    add x6, other arithmetic, masked_apply(): summed + lax.ppermute(summed, 'col', [(dev, dev ^ hop) for dev in range(8)])  70.3 us
  transfers between devices with their start and end apart: 12, of which 12 were waited for; matrix products, arithmetic and copies ran while one was open for 0% of the time, Pallas kernels for 0%

profile of v1, /device:TPU:0, one launch (start us, length us, event | category | flops | bytes accessed | tf_op | source)
XLA Modules:
  0.0 2276.5 jit_solution(11100113205738269379)
XLA Ops:
  6.5 9.6 copy.5
  16.2 9.6 copy.6
  25.7 11.9 convert_multiply_fusion
  37.7 4.8 dynamic-slice_select_fusion.2
  42.5 0.5 all-reduce.9.cloned.1.call-start
  43.0 174.3 %all-reduce.7.cloned.1.call-done = f32[2304,512]{0,1:T(8,128)} async-done(((f32[2304,512]{0,1:T(8,128)}), f32[2304,512]{0,1:T(8,128)}) %all-reduce.7.cloned.1.call-update) | async-done | bytes 4718608 | tf_op jit(solution)/shard_map/psum | solution.py:12
  217.3 75.4 %convolution_bitcast_fusion.2 = f32[4608,512]{0,1:T(8,128)S(1)} fusion(f32[2304,512]{0,1:T(8,128)} %all-reduce.7.cloned.1.call-done, f32[4608,2304]{1,0:T(8,128)} %param.4), kind=kOutput, calls=%fused_computation.14 | convolution fusion | flops 65229815808 | bytes 56623104 | tf_op jit(solution)/shard_map/dot_general | solution.py:35
  292.8 3.6 copy-done.1
  296.4 14.8 collective-permute-done
  311.2 11.8 add.98
  323.0 1.5 collective-permute-start.1
  324.5 203.8 %collective-permute-done.1 = f32[4608,512]{0,1:T(8,128)} collective-permute-done((f32[4608,512]{0,1:T(8,128)}, f32[4608,512]{0,1:T(8,128)}, u32[]{:S(2)}, u32[]{:S(2)}) %collective-permute-start.1) | collective-permute-done | bytes 9437216 | tf_op jit(solution)/shard_map/ppermute | solution.py:43
  528.3 11.8 add.99
  540.1 1.5 collective-permute-start.2
  542.2 202.2 %collective-permute-done.2 = f32[4608,512]{0,1:T(8,128)S(1)} collective-permute-done((f32[4608,512]{0,1:T(8,128)}, f32[4608,512]{0,1:T(8,128)S(1)}, u32[]{:S(2)}, u32[]{:S(2)}) %collective-permute-start.2) | collective-permute-done | bytes 9437216 | tf_op jit(solution)/shard_map/ppermute | solution.py:43
  744.4 14.1 multiply_reduce_fusion.4
  758.5 9.4 all-reduce.2
  767.9 12.5 multiply_subtract_fusion.1
  780.4 4.8 dynamic-slice_select_fusion.1
  785.5 170.5 %all-reduce.9.cloned.1.call-done = f32[2304,512]{0,1:T(8,128)} async-done(((f32[2304,512]{0,1:T(8,128)}), f32[2304,512]{0,1:T(8,128)}) %all-reduce.9.cloned.1.call-update) | async-done | bytes 4718608 | tf_op jit(solution)/shard_map/psum | solution.py:12
  956.0 75.4 %convolution_bitcast_fusion.1 = f32[4608,512]{0,1:T(8,128)S(1)} fusion(f32[2304,512]{0,1:T(8,128)} %all-reduce.9.cloned.1.call-done, f32[4608,2304]{1,0:T(8,128)} %param.4), kind=kOutput, calls=%fused_computation.13 | convolution fusion | flops 65229815808 | bytes 56623104 | tf_op jit(solution)/shard_map/dot_general | solution.py:35
  1031.4 3.6 copy-done.2
  1035.0 14.8 collective-permute-done.3
  1049.8 11.7 add.103
  1061.5 1.5 collective-permute-start.4
  1062.9 203.8 %collective-permute-done.4 = f32[4608,512]{0,1:T(8,128)} collective-permute-done((f32[4608,512]{0,1:T(8,128)}, f32[4608,512]{0,1:T(8,128)}, u32[]{:S(2)}, u32[]{:S(2)}) %collective-permute-start.4) | collective-permute-done | bytes 9437216 | tf_op jit(solution)/shard_map/ppermute | solution.py:43
  1266.8 11.7 add.104
  1278.4 1.5 collective-permute-start.5
  1279.9 202.8 %collective-permute-done.5 = f32[4608,512]{0,1:T(8,128)S(1)} collective-permute-done((f32[4608,512]{0,1:T(8,128)}, f32[4608,512]{0,1:T(8,128)S(1)}, u32[]{:S(2)}, u32[]{:S(2)}) %collective-permute-start.5) | collective-permute-done | bytes 9437216 | tf_op jit(solution)/shard_map/ppermute | solution.py:43
  1482.8 13.8 multiply_reduce_fusion.2
  1496.5 9.6 all-reduce.1
  1506.2 15.7 multiply_subtract_fusion
  1521.9 3.7 copy-done
  1525.6 2.5 dynamic-slice_select_fusion
  1528.2 170.7 %all-reduce.11.cloned.1.call-done = f32[2304,512]{0,1:T(8,128)} async-done(((f32[2304,512]{0,1:T(8,128)}), f32[2304,512]{0,1:T(8,128)}) %all-reduce.11.cloned.1.call-update) | async-done | bytes 4718608 | tf_op jit(solution)/shard_map/psum | solution.py:12
  1698.8 75.4 %convolution_bitcast_fusion = f32[4608,512]{0,1:T(8,128)S(1)} fusion(f32[2304,512]{0,1:T(8,128)} %all-reduce.11.cloned.1.call-done, f32[4608,2304]{1,0:T(8,128)} %param.4), kind=kOutput, calls=%fused_computation.12 | convolution fusion | flops 65229815808 | bytes 56623104 | tf_op jit(solution)/shard_map/dot_general | solution.py:35
  1774.3 3.6 copy-done.3
  1777.9 14.8 collective-permute-done.6
  1792.6 11.7 add.112
  1804.3 1.5 collective-permute-start.7
  1805.8 203.8 %collective-permute-done.7 = f32[4608,512]{0,1:T(8,128)} collective-permute-done((f32[4608,512]{0,1:T(8,128)}, f32[4608,512]{0,1:T(8,128)}, u32[]{:S(2)}, u32[]{:S(2)}) %collective-permute-start.7) | collective-permute-done | bytes 9437216 | tf_op jit(solution)/shard_map/ppermute | solution.py:43
  2009.6 11.7 add.113
  2021.3 1.5 collective-permute-start.8
  2022.8 202.8 %collective-permute-done.8 = f32[4608,512]{0,1:T(8,128)S(1)} collective-permute-done((f32[4608,512]{0,1:T(8,128)}, f32[4608,512]{0,1:T(8,128)S(1)}, u32[]{:S(2)}, u32[]{:S(2)}) %collective-permute-start.8) | collective-permute-done | bytes 9437216 | tf_op jit(solution)/shard_map/ppermute | solution.py:43
  2225.6 10.3 multiply_reduce_fusion
  2236.0 9.4 all-reduce
  2245.4 14.8 multiply_add_fusion
  2260.2 9.6 copy.7
  (17 shorter events, 0.3 us)
Async XLA Ops:
  6.5 210.8 %all-reduce.7.cloned.1.call-start = ((), (), s32[]{:S(2)}) async-start(), calls=%async_computation | async-start | bytes 9437184 | tf_op jit(solution)/shard_map/psum | solution.py:12
  42.5 913.5 %all-reduce.9.cloned.1.call-start = ((), (), s32[]{:S(2)}) async-start(), calls=%async_computation.1 | async-start | bytes 9437184 | tf_op jit(solution)/shard_map/psum | solution.py:12
  292.7 3.7 copy-start.1
  296.4 14.8 collective-permute-start
  323.0 205.3 %collective-permute-start.1 = (f32[4608,512]{0,1:T(8,128)}, f32[4608,512]{0,1:T(8,128)}, u32[]{:S(2)}, u32[]{:S(2)}) collective-permute-start(f32[4608,512]{0,1:T(8,128)} %add.98), channel_id=1, source_target_pairs={{0,2},{1,3},{2,0},{3,1},{4,6},{5,7},{6,4},{7,5},{8,10},{9,11},{10,... | collective-permute-start | bytes 28311560 | tf_op jit(solution)/shard_map/ppermute | solution.py:43
  540.1 204.3 %collective-permute-start.2 = (f32[4608,512]{0,1:T(8,128)}, f32[4608,512]{0,1:T(8,128)S(1)}, u32[]{:S(2)}, u32[]{:S(2)}) collective-permute-start(f32[4608,512]{0,1:T(8,128)} %add.99), channel_id=1, source_target_pairs={{0,4},{1,5},{2,6},{3,7},{4,0},{5,1},{6,2},{7,3},{8,12},{9,13},{10,... | collective-permute-start | bytes 28311560 | tf_op jit(solution)/shard_map/ppermute | solution.py:43
  785.3 913.5 %all-reduce.11.cloned.1.call-start = ((), (), s32[]{:S(2)}) async-start(), calls=%async_computation.2 | async-start | bytes 9437184 | tf_op jit(solution)/shard_map/psum | solution.py:12
  1031.4 3.6 copy-start.2
  1035.0 14.8 collective-permute-start.3
  1061.5 205.3 %collective-permute-start.4 = (f32[4608,512]{0,1:T(8,128)}, f32[4608,512]{0,1:T(8,128)}, u32[]{:S(2)}, u32[]{:S(2)}) collective-permute-start(f32[4608,512]{0,1:T(8,128)} %add.103), channel_id=1, source_target_pairs={{0,2},{1,3},{2,0},{3,1},{4,6},{5,7},{6,4},{7,5},{8,10},{9,11},{10,... | collective-permute-start | bytes 28311560 | tf_op jit(solution)/shard_map/ppermute | solution.py:43
  1278.4 204.3 %collective-permute-start.5 = (f32[4608,512]{0,1:T(8,128)}, f32[4608,512]{0,1:T(8,128)S(1)}, u32[]{:S(2)}, u32[]{:S(2)}) collective-permute-start(f32[4608,512]{0,1:T(8,128)} %add.104), channel_id=1, source_target_pairs={{0,4},{1,5},{2,6},{3,7},{4,0},{5,1},{6,2},{7,3},{8,12},{9,13},{10,... | collective-permute-start | bytes 28311560 | tf_op jit(solution)/shard_map/ppermute | solution.py:43
  1482.8 13.8 copy-start.4
  1521.9 3.7 copy-start
  1774.2 3.6 copy-start.3
  1777.9 14.8 collective-permute-start.6
  1804.3 205.3 %collective-permute-start.7 = (f32[4608,512]{0,1:T(8,128)}, f32[4608,512]{0,1:T(8,128)}, u32[]{:S(2)}, u32[]{:S(2)}) collective-permute-start(f32[4608,512]{0,1:T(8,128)} %add.112), channel_id=1, source_target_pairs={{0,2},{1,3},{2,0},{3,1},{4,6},{5,7},{6,4},{7,5},{8,10},{9,11},{10,... | collective-permute-start | bytes 28311560 | tf_op jit(solution)/shard_map/ppermute | solution.py:43
  2021.3 204.3 %collective-permute-start.8 = (f32[4608,512]{0,1:T(8,128)}, f32[4608,512]{0,1:T(8,128)S(1)}, u32[]{:S(2)}, u32[]{:S(2)}) collective-permute-start(f32[4608,512]{0,1:T(8,128)} %add.113), channel_id=1, source_target_pairs={{0,4},{1,5},{2,6},{3,7},{4,0},{5,1},{6,2},{7,3},{8,12},{9,13},{10,... | collective-permute-start | bytes 28311560 | tf_op jit(solution)/shard_map/ppermute | solution.py:43
Sparse Core Ops, SparseCore 0:
  42.6 174.6 all-reduce.6
  785.4 170.5 all-reduce.8
  1528.3 170.5 all-reduce.10
